TPU v7x, 32 devices: a whole 2x2x4 slice. The times are simulated.
32 devices in a mesh: dp: 8 (over y, x, core), expert: 4 (over z).
Axes of the slice: x: 2, y: 2, z: 4, core: 2. Of those that a mesh axis runs over, the one named last changes fastest.
Arguments:
- tokens: bfloat16 [4096, 1536], P(('dp', 'expert')), may hold values from -6 to 6
- segment_ids: int32 [32, 128], P(('dp', 'expert')), may hold values from 0 to 3, never falling along the last dimension, each value on 1 to 64 neighbouring positions
- routes: int32 [4096, 8], P(('dp', 'expert')), may hold values from 0 to 19, as said below
- cotangent: bfloat16 [4096, 1536], P(('dp', 'expert')), may hold values from -6 to 6
- query_weight: bfloat16 [1536, 1536], P('dp'), may hold values from -0.15625 to 0.15625
- key_weight: bfloat16 [1536, 512], P('dp'), may hold values from -0.15625 to 0.15625
- value_matrix: bfloat16 [1536, 512], P('dp'), may hold values from -0.15625 to 0.15625
- out_weight: bfloat16 [1536, 1536], P('dp'), may hold values from -1.25 to 1.25
- first_gain: bfloat16 [1536], P('dp'), may hold values from 0.5 to 1.5
- second_gain: bfloat16 [1536], P('dp'), may hold values from 0.5 to 1.5
- router_weight: bfloat16 [1536, 20], P('dp'), may hold values from -0.078125 to 0.078125
- gate_weight: bfloat16 [20, 1536, 512], P('expert'), may hold values from -0.15625 to 0.15625
- up_weight: bfloat16 [20, 1536, 512], P('expert'), may hold values from -0.15625 to 0.15625
- down_weight: bfloat16 [20, 512, 1536], P('expert'), may hold values from -0.5 to 0.5
Outputs:
- layer_out: bfloat16 [4096, 1536], P(('dp', 'expert'))
- input_grad: float32 [4096, 1536], P(('dp', 'expert'))
- query_grad: float32 [1536, 1536], P('dp')
- key_grad: float32 [1536, 512], P('dp')
- value_grad: float32 [1536, 512], P('dp')
- out_grad: float32 [1536, 1536], P('dp')
- first_grad: float32 [1536], P('dp')
- second_grad: float32 [1536], P('dp')
- router_grad: float32 [1536, 20], P('dp')
- gate_grad: float32 [20, 1536, 512], P('expert', 'dp')
- up_grad: float32 [20, 1536, 512], P('expert', 'dp')
- down_grad: float32 [20, 512, 1536], P('expert', 'dp')
Inputs may be any that keep to these rules, and one draw needn't show every extreme that they name: `segment_ids`: within each row the segment ids start at 0, never fall and take 4 values; a sequence has at most 64 tokens and some sequence has exactly that many. `routes`: each token names 8 different experts. Among the 128 tokens of one device no expert is named more than 96 times; in every such block between four and eight experts are named exactly 96 times.
All inputs are finite; a program needn't handle non-finite values.
Results may differ from a plain program's by a relative error of at most 0.012.
Values may be sent and summed in bfloat16 or wider, within the bound.
No kernel may reach another device: no remote copies, remote signals or barrier semaphores. Data moves between devices by JAX's collectives and lax.ppermute only.
A program may use at most 256 MiB of HBM per device.

v0:
```python
import jax
import jax.numpy as jnp
from jax import lax
from jax.sharding import PartitionSpec as P

HEAD_SIZE = 64
CAP = 96
EPSILON = 1e-06
ROTARY_BASE = 10000.0
SCORE_FACTOR = 0.015625
HIGHEST = lax.Precision.HIGHEST


def rope_tables(positions, width):
    half = width // 2
    freq = ROTARY_BASE ** (-jnp.arange(half, dtype=jnp.float32) * 2.0 / width)
    angle = positions.astype(jnp.float32)[:, None] * freq[None, :]
    return (jnp.cos(angle)[:, None, :], jnp.sin(angle)[:, None, :])


def rotate(field, cosine, sine):
    half = field.shape[-1] // 2
    first, second = (field[..., :half], field[..., half:])
    return jnp.concatenate(
        [first * cosine - second * sine, second * cosine + first * sine], axis=-1
    )


def rotate_back(grad, cosine, sine):
    half = grad.shape[-1] // 2
    first, second = (grad[..., :half], grad[..., half:])
    return jnp.concatenate(
        [first * cosine + second * sine, second * cosine - first * sine], axis=-1
    )


def positions_of(segments):
    count = segments.shape[0]
    earlier = jnp.sum((segments[None, :] < segments[:, None]).astype(jnp.int32), axis=1)
    return jnp.arange(count, dtype=jnp.int32) - earlier


def attention_mask(segments):
    count = segments.shape[0]
    index = jnp.arange(count, dtype=jnp.int32)
    return (segments[:, None] == segments[None, :]) & (index[None, :] <= index[:, None])


def rms_forward(field, gain):
    inverse = lax.rsqrt(jnp.mean(field * field, axis=-1, keepdims=True) + EPSILON)
    return (inverse, field * inverse * gain.astype(jnp.float32))


def rms_backward(field, inverse, gain, grad):
    scaled = grad * gain.astype(jnp.float32)
    inner = jnp.mean(scaled * field, axis=-1, keepdims=True)
    return (inverse * scaled - field * inverse**3 * inner, jnp.sum(grad * field * inverse, axis=0))


def score_block(query_rows, key_rows, mask):
    score_matrix = (
        jnp.einsum("qean,wen->eaqw", query_rows, key_rows, preferred_element_type=jnp.float32)
        * SCORE_FACTOR
    )
    return jnp.where(mask[None, None], score_matrix, -1e30)


def expert_front(arrived, gate_weight, up_weight):
    gate_pre = jnp.einsum("erd,edh->erh", arrived, gate_weight, preferred_element_type=jnp.float32)
    up_pre = jnp.einsum("erd,edh->erh", arrived, up_weight, preferred_element_type=jnp.float32)
    hidden = (jax.nn.silu(gate_pre) * up_pre).astype(jnp.bfloat16)
    return (gate_pre, up_pre, hidden)


def local(
    tokens,
    segment_ids,
    routes,
    cotangent,
    query_weight,
    key_weight,
    value_matrix,
    out_weight,
    first_gain,
    second_gain,
    router_weight,
    gate_weight,
    up_weight,
    down_weight,
):
    gathered = (
        lax.all_gather(query_weight, "dp", axis=0, tiled=True),
        lax.all_gather(key_weight, "dp", axis=0, tiled=True),
        lax.all_gather(value_matrix, "dp", axis=0, tiled=True),
        lax.all_gather(out_weight, "dp", axis=0, tiled=True),
        lax.all_gather(first_gain, "dp", axis=0, tiled=True),
        lax.all_gather(second_gain, "dp", axis=0, tiled=True),
        lax.all_gather(router_weight, "dp", axis=0, tiled=True),
    )
    query_full, key_full, value_full, out_full, gain_one, gain_two, router_full = gathered
    token_rows, width = tokens.shape
    query_head_rows = query_full.shape[1] // HEAD_SIZE
    key_heads = key_full.shape[1] // HEAD_SIZE
    head_group = query_head_rows // key_heads
    experts = router_full.shape[1]
    choices_per = routes.shape[1]
    segments = segment_ids[0]
    mask = attention_mask(segments)
    cosine, sine = rope_tables(positions_of(segments), HEAD_SIZE)
    inputs = tokens.astype(jnp.float32)
    first_inverse, normed1 = rms_forward(inputs, gain_one)
    normed1 = normed1.astype(jnp.bfloat16)
    query_rows = rotate(
        jnp.dot(normed1, query_full, preferred_element_type=jnp.float32).reshape(
            token_rows, query_head_rows, HEAD_SIZE
        ),
        cosine,
        sine,
    )
    query_rows = query_rows.astype(jnp.bfloat16).reshape(
        token_rows, key_heads, head_group, HEAD_SIZE
    )
    key_rows = rotate(
        jnp.dot(normed1, key_full, preferred_element_type=jnp.float32).reshape(
            token_rows, key_heads, HEAD_SIZE
        ),
        cosine,
        sine,
    ).astype(jnp.bfloat16)
    value_rows = (
        jnp.dot(normed1, value_full, preferred_element_type=jnp.float32)
        .astype(jnp.bfloat16)
        .reshape(token_rows, key_heads, HEAD_SIZE)
    )
    score_matrix = score_block(query_rows, key_rows, mask)
    peak = jnp.max(score_matrix, axis=-1, keepdims=True)
    logsum = peak + jnp.log(jnp.sum(jnp.exp(score_matrix - peak), axis=-1, keepdims=True))
    probabilities = jnp.exp(score_matrix - logsum).astype(jnp.bfloat16)
    mixed_values = jnp.einsum(
        "wmik,kwy->iwmy", probabilities, value_rows, preferred_element_type=jnp.float32
    )
    mixed_values = mixed_values.astype(jnp.bfloat16).reshape(
        token_rows, query_head_rows * HEAD_SIZE
    )
    resid = inputs + jnp.dot(mixed_values, out_full, preferred_element_type=jnp.float32)
    second_inverse, normed2 = rms_forward(resid, gain_two)
    normed2 = normed2.astype(jnp.bfloat16)
    logits = jnp.dot(normed2, router_full, preferred_element_type=jnp.float32)
    choose = (routes[:, :, None] == jnp.arange(experts, dtype=jnp.int32)[None, None, :]).astype(
        jnp.float32
    )
    chosen = jnp.sum(choose * logits[:, None, :], axis=-1)
    top = jnp.max(chosen, axis=-1, keepdims=True)
    raised = jnp.exp(chosen - top)
    gates = raised / jnp.sum(raised, axis=-1, keepdims=True)
    flat = routes.reshape(-1)
    hits = (flat[:, None] == jnp.arange(experts, dtype=jnp.int32)[None, :]).astype(jnp.int32)
    slots = jnp.sum((jnp.cumsum(hits, axis=0) - hits) * hits, axis=1)
    empty = jnp.zeros((experts, CAP, width), jnp.bfloat16)
    outgoing = empty.at[flat, slots].set(jnp.repeat(normed2, choices_per, axis=0))
    arrived = lax.all_to_all(outgoing, "expert", split_axis=0, concat_axis=1, tiled=True)
    gate_pre, up_pre, hidden = expert_front(arrived, gate_weight, up_weight)
    produced = jnp.einsum(
        "erh,ehd->erd", hidden, down_weight, preferred_element_type=jnp.float32
    ).astype(jnp.bfloat16)
    returned = lax.all_to_all(produced, "expert", split_axis=1, concat_axis=0, tiled=True)
    picked = returned[flat, slots].reshape(token_rows, choices_per, width)
    combined = jnp.einsum("tk,tkd->td", gates, picked.astype(jnp.float32), precision=HIGHEST)
    layer_out = (resid + combined).astype(jnp.bfloat16)
    grad_out = cotangent.astype(jnp.float32)
    gate_back = jnp.einsum("td,tkd->tk", cotangent, picked, preferred_element_type=jnp.float32)
    chosen_back = gates * (gate_back - jnp.sum(gates * gate_back, axis=-1, keepdims=True))
    logit_back = jnp.sum(choose * chosen_back[:, :, None], axis=1)
    router_part = jnp.dot(normed2.astype(jnp.float32).T, logit_back, precision=HIGHEST)
    normed2_back = jnp.dot(logit_back, router_full.astype(jnp.float32).T, precision=HIGHEST)
    row_grads = (
        (gates[:, :, None] * grad_out[:, None, :])
        .astype(jnp.bfloat16)
        .reshape(token_rows * choices_per, width)
    )
    leaving = empty.at[flat, slots].set(row_grads)
    incoming = lax.all_to_all(leaving, "expert", split_axis=0, concat_axis=1, tiled=True)
    landed, gate_again, up_again, hidden_again = (arrived, gate_pre, up_pre, hidden)
    hidden_back = jnp.einsum(
        "erd,ehd->erh", incoming, down_weight, preferred_element_type=jnp.float32
    )
    sigma = jax.nn.sigmoid(gate_again)
    gate_rows = (hidden_back * up_again * sigma * (1.0 + gate_again * (1.0 - sigma))).astype(
        jnp.bfloat16
    )
    up_rows = (hidden_back * gate_again * sigma).astype(jnp.bfloat16)
    down_part = jnp.einsum(
        "erh,erd->ehd", hidden_again, incoming, preferred_element_type=jnp.float32
    )
    gate_part = jnp.einsum("erd,erh->edh", landed, gate_rows, preferred_element_type=jnp.float32)
    up_part = jnp.einsum("erd,erh->edh", landed, up_rows, preferred_element_type=jnp.float32)
    rows_back = jnp.einsum(
        "erh,edh->erd", gate_rows, gate_weight, preferred_element_type=jnp.float32
    )
    rows_back = (
        rows_back
        + jnp.einsum("erh,edh->erd", up_rows, up_weight, preferred_element_type=jnp.float32)
    ).astype(jnp.bfloat16)
    expert_sums = (gate_part, up_part, down_part)
    coming_back = lax.all_to_all(rows_back, "expert", split_axis=1, concat_axis=0, tiled=True)
    normed2_back = normed2_back + jnp.sum(
        coming_back[flat, slots].reshape(token_rows, choices_per, width).astype(jnp.float32), axis=1
    )
    resid_part, second_part = rms_backward(resid, second_inverse, gain_two, normed2_back)
    resid_back = grad_out + resid_part
    attended_back = resid_back.astype(jnp.bfloat16)
    out_part = jnp.dot(mixed_values.T, attended_back, preferred_element_type=jnp.float32)
    mixed_values_gradient = jnp.dot(
        attended_back, out_full.T, preferred_element_type=jnp.float32
    ).astype(jnp.bfloat16)
    mixed_values_gradient = mixed_values_gradient.reshape(
        token_rows, key_heads, head_group, HEAD_SIZE
    )
    second_pass = jnp.exp(score_block(query_rows, key_rows, mask) - logsum)
    value_rows_gradient = jnp.einsum(
        "kjal,akjx->lkx",
        second_pass.astype(jnp.bfloat16),
        mixed_values_gradient,
        preferred_element_type=jnp.float32,
    )
    probability_gradient = jnp.einsum(
        "qean,wen->eaqw", mixed_values_gradient, value_rows, preferred_element_type=jnp.float32
    )
    delta = jnp.sum(second_pass * probability_gradient, axis=-1, keepdims=True)
    score_gradient = (second_pass * (probability_gradient - delta) * SCORE_FACTOR).astype(
        jnp.bfloat16
    )
    query_rows_gradient = jnp.einsum(
        "wmik,kwy->iwmy", score_gradient, key_rows, preferred_element_type=jnp.float32
    ).reshape(token_rows, query_head_rows, HEAD_SIZE)
    key_rows_gradient = jnp.einsum(
        "kjal,akjx->lkx", score_gradient, query_rows, preferred_element_type=jnp.float32
    )
    query_rows_gradient = (
        rotate_back(query_rows_gradient, cosine, sine)
        .astype(jnp.bfloat16)
        .reshape(token_rows, query_head_rows * HEAD_SIZE)
    )
    key_rows_gradient = (
        rotate_back(key_rows_gradient, cosine, sine)
        .astype(jnp.bfloat16)
        .reshape(token_rows, key_heads * HEAD_SIZE)
    )
    value_rows_gradient = value_rows_gradient.astype(jnp.bfloat16).reshape(
        token_rows, key_heads * HEAD_SIZE
    )
    query_part = jnp.dot(normed1.T, query_rows_gradient, preferred_element_type=jnp.float32)
    key_part = jnp.dot(normed1.T, key_rows_gradient, preferred_element_type=jnp.float32)
    value_part = jnp.dot(normed1.T, value_rows_gradient, preferred_element_type=jnp.float32)
    normed1_back = jnp.dot(query_rows_gradient, query_full.T, preferred_element_type=jnp.float32)
    normed1_back = normed1_back + jnp.dot(
        key_rows_gradient, key_full.T, preferred_element_type=jnp.float32
    )
    normed1_back = normed1_back + jnp.dot(
        value_rows_gradient, value_full.T, preferred_element_type=jnp.float32
    )
    input_part, first_part = rms_backward(inputs, first_inverse, gain_one, normed1_back)
    input_grad = resid_back + input_part
    partial_sums = (
        lax.psum_scatter(query_part, "dp", scatter_dimension=0, tiled=True),
        lax.psum_scatter(key_part, "dp", scatter_dimension=0, tiled=True),
        lax.psum_scatter(value_part, "dp", scatter_dimension=0, tiled=True),
        lax.psum_scatter(out_part, "dp", scatter_dimension=0, tiled=True),
        lax.psum_scatter(first_part, "dp", scatter_dimension=0, tiled=True),
        lax.psum_scatter(second_part, "dp", scatter_dimension=0, tiled=True),
        lax.psum_scatter(router_part, "dp", scatter_dimension=0, tiled=True),
    )
    totals = lax.psum(
        (
            partial_sums[0],
            partial_sums[1],
            partial_sums[2],
            partial_sums[3],
            partial_sums[4],
            partial_sums[5],
            partial_sums[6],
        ),
        "expert",
    )
    expert_sums = (
        lax.psum_scatter(gate_part, "dp", scatter_dimension=1, tiled=True),
        lax.psum_scatter(up_part, "dp", scatter_dimension=1, tiled=True),
        lax.psum_scatter(down_part, "dp", scatter_dimension=1, tiled=True),
    )
    return (
        layer_out,
        input_grad,
        totals[0],
        totals[1],
        totals[2],
        totals[3],
        totals[4],
        totals[5],
        totals[6],
        expert_sums[0],
        expert_sums[1],
        expert_sums[2],
    )


def solution(mesh):
    return jax.shard_map(
        local,
        mesh=mesh,
        in_specs=(
            P(("dp", "expert"), None),
            P(("dp", "expert"), None),
            P(("dp", "expert"), None),
            P(("dp", "expert"), None),
            P("dp", None),
            P("dp", None),
            P("dp", None),
            P("dp", None),
            P("dp"),
            P("dp"),
            P("dp", None),
            P("expert", None, None),
            P("expert", None, None),
            P("expert", None, None),
        ),
        out_specs=(
            P(("dp", "expert"), None),
            P(("dp", "expert"), None),
            P("dp", None),
            P("dp", None),
            P("dp", None),
            P("dp", None),
            P("dp"),
            P("dp"),
            P("dp", None),
            P("expert", "dp", None),
            P("expert", "dp", None),
            P("expert", "dp", None),
        ),
        check_vma=False,
    )
```

profile of v0, /device:TPU:0, one launch (start us, length us, event | category | flops | bytes accessed | tf_op | source)
XLA Modules:
  0.0 1799.5 jit_solution(2375361750178085493)
XLA Ops:
  14.8 15.5 all-reduce.7
  40.5 25.7 %all-gather.8.cloned.1.call-done = bf16[1536,512]{1,0:T(8,128)(2,1)} async-done(((bf16[192,512]{1,0:T(8,128)(2,1)}), bf16[1536,512]{1,0:T(8,128)(2,1)}) %all-gather.8.cloned.1.call-update) | async-done | bytes 1572880 | tf_op jit(solution)/shard_map/all_gather | solution.py:93
  68.4 38.6 %all-gather.10.cloned.1.call-done = bf16[1536,1536]{1,0:T(8,128)(2,1)} async-done(((bf16[192,1536]{1,0:T(8,128)(2,1)}), bf16[1536,1536]{1,0:T(8,128)(2,1)}) %all-gather.10.cloned.1.call-update) | async-done | bytes 4718608 | tf_op jit(solution)/shard_map/all_gather | solution.py:92
  114.2 33.5 %all-gather.12.cloned.1.call-done = bf16[1536,1536]{1,0:T(8,128)(2,1)} async-done(((bf16[192,1536]{1,0:T(8,128)(2,1)}), bf16[1536,1536]{1,0:T(8,128)(2,1)}) %all-gather.12.cloned.1.call-update) | async-done | bytes 4718608 | tf_op jit(solution)/shard_map/all_gather | solution.py:95
  161.5 134.7 %all_to_all.72 = bf16[20,96,1536]{2,1,0:T(8,128)(2,1)S(1)} all-to-all(bf16[20,96,1536]{2,1,0:T(8,128)(2,1)} %bitcast.191), channel_id=1, replica_groups=mesh['dp'=8,'expert'=4] {'expert'}, dimensions={0} | all-to-all | bytes 11796480 | tf_op jit(solution)/shard_map/all_to_all | solution.py:161
  350.4 193.8 %all-to-all-done.1 = bf16[5,384,1536]{2,0,1:T(8,128)(2,1)} async-done(((bf16[5,384,1536]{2,0,1:T(8,128)(2,1)}), bf16[5,384,1536]{2,0,1:T(8,128)(2,1)}, u32[]{:S(2)}, u32[]{:S(2)}) %all-to-all-start.1) | async-done | bytes 5898272 | tf_op jit(solution)/shard_map/all_to_all | solution.py:166
  552.7 17.8 gather_fusion
  586.2 133.4 %all_to_all.73 = bf16[20,96,1536]{2,1,0:T(8,128)(2,1)S(1)} all-to-all(bf16[20,96,1536]{2,1,0:T(8,128)(2,1)} %bitcast.188), channel_id=1, replica_groups=mesh['dp'=8,'expert'=4] {'expert'}, dimensions={0} | all-to-all | bytes 11796480 | tf_op jit(solution)/shard_map/all_to_all | solution.py:182
  722.7 12.6 multiply_convert_fusion
  746.5 13.0 add_convert_fusion
  781.5 198.6 %all-to-all-done.3 = bf16[5,384,1536]{2,0,1:T(8,128)(2,1)} async-done(((bf16[5,384,1536]{2,0,1:T(8,128)(2,1)}), bf16[5,384,1536]{2,0,1:T(8,128)(2,1)}, u32[]{:S(2)}, u32[]{:S(2)}) %all-to-all-start.3) | async-done | bytes 5898272 | tf_op jit(solution)/shard_map/all_to_all | solution.py:205
  988.5 23.3 %gather_fusion.1 = bf16[1024,1536]{1,0:T(8,128)(2,1)} fusion(bf16[20,96,1536]{2,1,0:T(8,128)(2,1)} %bitcast.181, s32[1024]{0:T(1024)S(1)} %bitcast.179), kind=kCustom, calls=%fused_computation.1 | custom fusion | bytes 6299648 | tf_op jit(solution)/shard_map/gather | solution.py:207
  1060.3 13.1 fusion.83
  1073.6 13.9 fusion.82
  1099.0 24.6 %reduce-scatter.13.cloned.1.call-done = f32[192,512]{1,0:T(8,128)} async-done(((f32[1536,512]{1,0:T(8,128)}), f32[192,512]{1,0:T(8,128)}) %reduce-scatter.13.cloned.1.call-update) | async-done | bytes 393232 | tf_op jit(solution)/shard_map/reduce_scatter | solution.py:266
  1123.6 80.0 %reduce-scatter.17.cloned.1.call-done = f32[192,1536]{1,0:T(8,128)} async-done(((f32[1536,1536]{1,0:T(8,128)}), f32[192,1536]{1,0:T(8,128)}) %reduce-scatter.17.cloned.1.call-update) | async-done | bytes 1179664 | tf_op jit(solution)/shard_map/reduce_scatter | solution.py:268
  1203.6 80.0 %reduce-scatter.11.cloned.1.call-done = f32[192,1536]{1,0:T(8,128)} async-done(((f32[1536,1536]{1,0:T(8,128)}), f32[192,1536]{1,0:T(8,128)}) %reduce-scatter.11.cloned.1.call-update) | async-done | bytes 1179664 | tf_op jit(solution)/shard_map/reduce_scatter | solution.py:265
  1284.5 37.9 %reduce-scatter.25.cloned.1.call-done = f32[192,20]{1,0:T(8,128)} async-done(((f32[1536,20]{1,0:T(8,128)}), f32[192,20]{1,0:T(8,128)}) %reduce-scatter.25.cloned.1.call-update) | async-done | bytes 15376
  1329.1 22.8 %all-reduce.4 = (f32[1536]{0:T(1024)S(1)}, f32[1536]{0:T(1024)S(1)}) all-reduce(f32[1536]{0:T(1024)S(1)} %get-tuple-element.14, f32[1536]{0:T(1024)S(1)} %copy-done.47), channel_id=6, replica_groups=mesh['dp'=8,'expert'=4] {'dp'}, use_global_device_ids=true, to_apply=%region_28.29.clone | all-reduce | flops 3072 | bytes 24576
  1352.0 19.6 %all-reduce.5 = (f32[192]{0:T(256)}, f32[192]{0:T(256)}, f32[192,20]{0,1:T(8,128)}) all-reduce(f32[192]{0:T(256)S(1)} %dynamic-slice.3, f32[192]{0:T(256)S(1)} %dynamic-slice.5, f32[192,20]{0,1:T(8,128)S(1)} %copy.139), channel_id=1, replica_groups=mesh['dp'=8,'expert'=4] {'expert'}, use_global_device_ids=true, to_apply=%region_29.30 | all-reduce | flops 4224 | bytes 33792 | tf_op jit(solution)/shard_map/psum | solution.py:273
  1372.8 62.7 %reduce-scatter.23.cloned.1.call-done = f32[5,64,1536]{2,1,0:T(8,128)} async-done(((f32[5,512,1536]{2,1,0:T(8,128)}), f32[5,64,1536]{2,1,0:T(8,128)}) %reduce-scatter.23.cloned.1.call-update) | async-done | bytes 1966096 | tf_op jit(solution)/shard_map/reduce_scatter | solution.py:288
  1435.5 113.3 %reduce-scatter.21.cloned.1.call-done = f32[5,192,512]{2,1,0:T(8,128)} async-done(((f32[5,1536,512]{2,1,0:T(8,128)}), f32[5,192,512]{2,1,0:T(8,128)}) %reduce-scatter.21.cloned.1.call-update) | async-done | bytes 1966096 | tf_op jit(solution)/shard_map/reduce_scatter | solution.py:287
  1548.8 113.1 %reduce-scatter.19.cloned.1.call-done = f32[5,192,512]{2,1,0:T(8,128)} async-done(((f32[5,1536,512]{2,1,0:T(8,128)}), f32[5,192,512]{2,1,0:T(8,128)}) %reduce-scatter.19.cloned.1.call-update) | async-done | bytes 1966096 | tf_op jit(solution)/shard_map/reduce_scatter | solution.py:286
  1661.9 124.8 %all-reduce.10.cloned.1.call-done = (f32[192,1536]{1,0:T(8,128)}, f32[192,512]{1,0:T(8,128)}, f32[192,512]{1,0:T(8,128)}, f32[192,1536]{1,0:T(8,128)}) async-done(((f32[192,1536]{1,0:T(8,128)}, f32[192,512]{1,0:T(8,128)}, f32[192,512]{1,0:T(8,128)}, f32[192,1536]{1,0:T(8,128)}), (f32[192,1536]{1,0:T(8,128)}, f32[192,512]{1,0:T(8,128)}, f32[192,512]{1,0:T(8,128)}, ...) | async-done | bytes 3145744 | tf_op jit(solution)/shard_map/psum | solution.py:273
  (262 shorter events, 236.9 us)
Async XLA Ops:
  7.2 31.3 %all-gather.6.cloned.1.call-start = ((), (), s32[]{:S(2)}) async-start(), calls=%async_computation.12 | async-start | bytes 1769472 | tf_op jit(solution)/shard_map/all_gather | solution.py:94
  8.0 58.2 %all-gather.8.cloned.1.call-start = ((), (), s32[]{:S(2)}) async-start(), calls=%async_computation.13 | async-start | bytes 1769472 | tf_op jit(solution)/shard_map/all_gather | solution.py:93
  8.7 98.3 %all-gather.10.cloned.1.call-start = ((), (), s32[]{:S(2)}) async-start(), calls=%async_computation.14 | async-start | bytes 5308416 | tf_op jit(solution)/shard_map/all_gather | solution.py:92
  9.4 138.2 %all-gather.12.cloned.1.call-start = ((), (), s32[]{:S(2)}) async-start(), calls=%async_computation.15 | async-start | bytes 5308416 | tf_op jit(solution)/shard_map/all_gather | solution.py:95
  30.4 121.2 %copy-start.37 = (f32[1536]{0:T(1024)}, f32[1536]{0:T(1024)S(1)}, u32[]{:S(2)}) copy-start(f32[1536]{0:T(1024)S(1)} %convert_element_type.119) | copy-start | bytes 18436
  37.7 73.7 %copy-start.48 = (f32[128]{0:T(128)}, f32[128]{0:T(128)S(1)}, u32[]{:S(2)}) copy-start(f32[128]{0:T(128)S(1)} %get-tuple-element.49) | copy-start | bytes 1540
  37.7 114.3 %copy-start.54 = (s32[1024]{0:T(1024)}, s32[1024]{0:T(1024)S(1)}, u32[]{:S(2)}) copy-start(s32[1024]{0:T(1024)S(1)} %broadcast_select_fusion) | copy-start | bytes 12292
  37.9 73.5 %copy-start.26 = (f32[128,32]{0,1:T(8,128)}, f32[128,32]{0,1:T(8,128)S(1)}, u32[]{:S(2)}) copy-start(f32[128,32]{0,1:T(8,128)S(1)} %get-tuple-element.44) | copy-start | bytes 49156
  152.0 197.6 %copy-start.7 = (bf16[128,1536]{1,0:T(8,128)(2,1)}, bf16[128,1536]{1,0:T(8,128)(2,1)S(1)}, u32[]{:S(2)}) copy-start(bf16[128,1536]{1,0:T(8,128)(2,1)S(1)} %multiply_convert_fusion.3) | copy-start | bytes 1179652
  333.1 211.1 %all-to-all-start.1 = ((bf16[5,384,1536]{2,0,1:T(8,128)(2,1)}), bf16[5,384,1536]{2,0,1:T(8,128)(2,1)}, u32[]{:S(2)}, u32[]{:S(2)}) async-start(bf16[5,384,1536]{2,0,1:T(8,128)(2,1)} %copy.108), calls=%async_computation.1 | async-start | bytes 18874368 | tf_op jit(solution)/shard_map/all_to_all | solution.py:166
  348.6 204.1 %copy-start.24 = (bf16[1536,20]{0,1:T(8,128)(2,1)}, bf16[1536,20]{0,1:T(8,128)(2,1)S(1)}, u32[]{:S(2)}) copy-start(bf16[1536,20]{0,1:T(8,128)(2,1)S(1)} %reshape.368) | copy-start | bytes 184324
  349.8 202.9 %copy-start.53 = (f32[128]{0:T(128)}, f32[128]{0:T(128)S(1)}, u32[]{:S(2)}) copy-start(f32[128]{0:T(128)S(1)} %reduce_max.19) | copy-start | bytes 1540
  769.4 210.6 %all-to-all-start.3 = ((bf16[5,384,1536]{2,0,1:T(8,128)(2,1)}), bf16[5,384,1536]{2,0,1:T(8,128)(2,1)}, u32[]{:S(2)}, u32[]{:S(2)}) async-start(bf16[5,384,1536]{2,0,1:T(8,128)(2,1)} %copy.112), calls=%async_computation.3 | async-start | bytes 18874368 | tf_op jit(solution)/shard_map/all_to_all | solution.py:205
  775.4 323.6 %reduce-scatter.15.cloned.1.call-start = ((), (), s32[]{:S(2)}) async-start(), calls=%async_computation.18 | async-start | bytes 3538944 | tf_op jit(solution)/shard_map/reduce_scatter | solution.py:267
  776.0 239.9 %copy-start.39 = (f32[128,20]{0,1:T(8,128)}, f32[128,20]{0,1:T(8,128)S(1)}, u32[]{:S(2)}) copy-start(f32[128,20]{0,1:T(8,128)S(1)} %select_reduce_fusion) | copy-start | bytes 30724
  1029.3 94.4 %reduce-scatter.13.cloned.1.call-start = ((), (), s32[]{:S(2)}) async-start(), calls=%async_computation.17 | async-start | bytes 3538944 | tf_op jit(solution)/shard_map/reduce_scatter | solution.py:266
  1039.4 164.2 %reduce-scatter.17.cloned.1.call-start = ((), (), s32[]{:S(2)}) async-start(), calls=%async_computation.19 | async-start | bytes 10616832 | tf_op jit(solution)/shard_map/reduce_scatter | solution.py:268
  1044.5 239.2 %reduce-scatter.11.cloned.1.call-start = ((), (), s32[]{:S(2)}) async-start(), calls=%async_computation.16 | async-start | bytes 10616832 | tf_op jit(solution)/shard_map/reduce_scatter | solution.py:265
  1057.1 265.3 %reduce-scatter.25.cloned.1.call-start = ((), (), s32[]{:S(2)}) async-start(), calls=%async_computation.23 | async-start | bytes 884736
  1060.2 375.3 %reduce-scatter.23.cloned.1.call-start = ((), (), s32[]{:S(2)}) async-start(), calls=%async_computation.22 | async-start | bytes 17694720 | tf_op jit(solution)/shard_map/reduce_scatter | solution.py:288
  1073.3 475.4 %reduce-scatter.21.cloned.1.call-start = ((), (), s32[]{:S(2)}) async-start(), calls=%async_computation.21 | async-start | bytes 17694720 | tf_op jit(solution)/shard_map/reduce_scatter | solution.py:287
  1087.5 574.4 %reduce-scatter.19.cloned.1.call-start = ((), (), s32[]{:S(2)}) async-start(), calls=%async_computation.20 | async-start | bytes 17694720 | tf_op jit(solution)/shard_map/reduce_scatter | solution.py:286
  1098.9 224.5 %copy-start.12 = (bf16[128,24,64]{0,2,1:T(8,128)(2,1)S(1)}, bf16[128,24,64]{0,2,1:T(8,128)(2,1)}, u32[]{:S(2)}) copy-start(bf16[128,24,64]{0,2,1:T(8,128)(2,1)} %copy-done.11) | copy-start | bytes 1179652
  1098.9 687.8 %all-reduce.10.cloned.1.call-start = ((), (), s32[]{:S(2)}) async-start(), calls=%async_computation.24 | async-start | bytes 6291456 | tf_op jit(solution)/shard_map/psum | solution.py:273
  (53 other events, 720.5 us)
Sparse Core Ops, SparseCore 0:
  9.9 28.5 all-gather.5
  40.4 25.7 all-gather.7
  68.0 38.9 all-gather.9
  108.7 38.9 all-gather.11
  1029.4 44.3 reduce-scatter.14
  1077.4 46.2 reduce-scatter.12
  1127.1 76.4 reduce-scatter.16
  1207.1 76.4 reduce-scatter.10
  1287.4 34.9 reduce-scatter.24
  1326.3 109.1 reduce-scatter.22
  1439.6 109.1 reduce-scatter.20
  1552.7 109.1 reduce-scatter.18
  1664.5 122.1 all-reduce.9
where the time goes:
time: 1810 us; the launch traced here: 1800 us
  waiting for transfers between devices  1130 us (62%)
  blocking collectives  335 us (19%)
  matrix products  165 us (9%)
  local copies, waits for them, and re-layouts  112 us (6%)
  other arithmetic  27.9 us (2%)
    all_to_all x1, waiting for transfers between devices, local(): lax.all_to_all(rows_back, 'expert', split_axis=1, concat_axis=0, tiled=True)  199 us
    all_to_all x1, waiting for transfers between devices, local(): lax.all_to_all(produced, 'expert', split_axis=1, concat_axis=0, tiled=True)  194 us
    all_to_all x1, blocking collectives, local(): lax.all_to_all(outgoing, 'expert', split_axis=0, concat_axis=1, tiled=True)  135 us
    all_to_all x1, blocking collectives, local(): lax.all_to_all(leaving, 'expert', split_axis=0, concat_axis=1, tiled=True)  133 us
    psum x1, waiting for transfers between devices, local(): lax.psum((partial_sums[0], partial_sums[1], partial_sums[2], partial_sums...  125 us
    reduce_scatter x1, waiting for transfers between devices, local(): lax.psum_scatter(up_part, 'dp', scatter_dimension=1, tiled=True)  113 us
    reduce_scatter x1, waiting for transfers between devices, local(): lax.psum_scatter(gate_part, 'dp', scatter_dimension=1, tiled=True)  113 us
    reduce_scatter x1, waiting for transfers between devices, local(): lax.psum_scatter(query_part, 'dp', scatter_dimension=0, tiled=True)  80 us
  transfers between devices with their start and end apart: 15, of which 14 were waited for; matrix products, arithmetic and copies ran while one was open for 6% of the time, Pallas kernels for 0%

commit v1 on v0

--- a/solution.py
+++ b/solution.py
@@ -163,7 +163,15 @@
     produced = jnp.einsum(
         "erh,ehd->erd", hidden, down_weight, preferred_element_type=jnp.float32
     ).astype(jnp.bfloat16)
-    returned = lax.all_to_all(produced, "expert", split_axis=1, concat_axis=0, tiled=True)
+
+    def _watch_modes(block_here):
+        block_now = lax.axis_size("expert")
+        moved = jnp.split(block_here, block_now, 1)
+        clean = jnp.stack(moved, axis=0)
+        y_new = lax.all_to_all(clean, axis_name="expert", split_axis=0, concat_axis=0)
+        return jnp.concatenate(y_new, 0)
+
+    returned = _watch_modes(produced)
     picked = returned[flat, slots].reshape(token_rows, choices_per, width)
     combined = jnp.einsum("tk,tkd->td", gates, picked.astype(jnp.float32), precision=HIGHEST)
     layer_out = (resid + combined).astype(jnp.bfloat16)

time: 1810 us -> 1720 us (0.950)
  waiting for transfers between devices: 1130 us -> 1050 us
  local copies, waits for them, and re-layouts: 112 us -> 93.7 us
    all_to_all x1, waiting for transfers between devices: 194 us -> 118 us  [_watch_modes(): lax.all_to_all(clean, axis_name='expert', split_axis=0, concat_axis=0)]
where the time goes in v1:
time: 1720 us; the launch traced here: 1710 us
  waiting for transfers between devices  1050 us (61%)
  blocking collectives  335 us (19%)
  matrix products  163 us (9%)
  local copies, waits for them, and re-layouts  93.7 us (5%)
  other arithmetic  31.1 us (2%)
    all_to_all x1, waiting for transfers between devices, local(): lax.all_to_all(rows_back, 'expert', split_axis=1, concat_axis=0, tiled=True)  199 us
    all_to_all x1, blocking collectives, local(): lax.all_to_all(outgoing, 'expert', split_axis=0, concat_axis=1, tiled=True)  135 us
    all_to_all x1, blocking collectives, local(): lax.all_to_all(leaving, 'expert', split_axis=0, concat_axis=1, tiled=True)  133 us
    psum x1, waiting for transfers between devices, local(): lax.psum((partial_sums[0], partial_sums[1], partial_sums[2], partial_sums...  125 us
    all_to_all x1, waiting for transfers between devices, _watch_modes(): lax.all_to_all(clean, axis_name='expert', split_axis=0, concat_axis=0)  118 us
    reduce_scatter x1, waiting for transfers between devices, local(): lax.psum_scatter(up_part, 'dp', scatter_dimension=1, tiled=True)  113 us
    reduce_scatter x1, waiting for transfers between devices, local(): lax.psum_scatter(gate_part, 'dp', scatter_dimension=1, tiled=True)  113 us
    reduce_scatter x1, waiting for transfers between devices, local(): lax.psum_scatter(out_part, 'dp', scatter_dimension=0, tiled=True)  80 us
  transfers between devices with their start and end apart: 15, of which 14 were waited for; matrix products, arithmetic and copies ran while one was open for 6% of the time, Pallas kernels for 0%

profile of v1, /device:TPU:0, one launch (start us, length us, event | category | flops | bytes accessed | tf_op | source)
XLA Modules:
  0.0 1706.6 jit_solution(9802376331697893075)
XLA Ops:
  14.8 15.5 all-reduce.7
  40.5 25.7 %all-gather.8.cloned.1.call-done = bf16[1536,512]{1,0:T(8,128)(2,1)} async-done(((bf16[192,512]{1,0:T(8,128)(2,1)}), bf16[1536,512]{1,0:T(8,128)(2,1)}) %all-gather.8.cloned.1.call-update) | async-done | bytes 1572880 | tf_op jit(solution)/shard_map/all_gather | solution.py:93
  68.4 38.6 %all-gather.10.cloned.1.call-done = bf16[1536,1536]{1,0:T(8,128)(2,1)} async-done(((bf16[192,1536]{1,0:T(8,128)(2,1)}), bf16[1536,1536]{1,0:T(8,128)(2,1)}) %all-gather.10.cloned.1.call-update) | async-done | bytes 4718608 | tf_op jit(solution)/shard_map/all_gather | solution.py:92
  114.2 33.5 %all-gather.12.cloned.1.call-done = bf16[1536,1536]{1,0:T(8,128)(2,1)} async-done(((bf16[192,1536]{1,0:T(8,128)(2,1)}), bf16[1536,1536]{1,0:T(8,128)(2,1)}) %all-gather.12.cloned.1.call-update) | async-done | bytes 4718608 | tf_op jit(solution)/shard_map/all_gather | solution.py:95
  161.5 134.7 %all_to_all.59 = bf16[20,96,1536]{2,1,0:T(8,128)(2,1)S(1)} all-to-all(bf16[20,96,1536]{2,1,0:T(8,128)(2,1)} %bitcast.195), channel_id=1, replica_groups=mesh['dp'=8,'expert'=4] {'expert'}, dimensions={0} | all-to-all | bytes 11796480 | tf_op jit(solution)/shard_map/all_to_all | solution.py:161
  341.9 117.9 %all-to-all-done.1 = bf16[4,5,96,1536]{3,2,1,0:T(8,128)(2,1)} async-done(((bf16[4,5,96,1536]{3,2,1,0:T(8,128)(2,1)}), bf16[4,5,96,1536]{3,2,1,0:T(8,128)(2,1)}, u32[]{:S(2)}, u32[]{:S(2)}) %all-to-all-start.1) | async-done | bytes 5898272 | tf_op jit(solution)/shard_map/all_to_all | solution.py:171
  459.9 17.8 %gather_fusion = bf16[1024,1536]{1,0:T(8,128)(2,1)S(1)} fusion(bf16[20,96,1536]{2,1,0:T(8,128)(2,1)} %bitcast.28, s32[1024]{0:T(1024)S(1)} %bitcast.183), kind=kCustom, calls=%fused_computation | custom fusion | bytes 6299648 | tf_op jit(solution)/shard_map/gather | solution.py:175
  493.4 133.4 %all_to_all.60 = bf16[20,96,1536]{2,1,0:T(8,128)(2,1)S(1)} all-to-all(bf16[20,96,1536]{2,1,0:T(8,128)(2,1)} %bitcast.192), channel_id=1, replica_groups=mesh['dp'=8,'expert'=4] {'expert'}, dimensions={0} | all-to-all | bytes 11796480 | tf_op jit(solution)/shard_map/all_to_all | solution.py:190
  629.9 12.5 multiply_convert_fusion
  653.6 13.0 add_convert_fusion
  688.5 198.6 %all-to-all-done.3 = bf16[5,384,1536]{2,0,1:T(8,128)(2,1)} async-done(((bf16[5,384,1536]{2,0,1:T(8,128)(2,1)}), bf16[5,384,1536]{2,0,1:T(8,128)(2,1)}, u32[]{:S(2)}, u32[]{:S(2)}) %all-to-all-start.3) | async-done | bytes 5898272 | tf_op jit(solution)/shard_map/all_to_all | solution.py:213
  895.6 23.3 %gather_fusion.1 = bf16[1024,1536]{1,0:T(8,128)(2,1)} fusion(bf16[20,96,1536]{2,1,0:T(8,128)(2,1)} %bitcast.185, s32[1024]{0:T(1024)S(1)} %bitcast.184), kind=kCustom, calls=%fused_computation.1 | custom fusion | bytes 6299648 | tf_op jit(solution)/shard_map/gather | solution.py:215
  967.3 13.1 fusion.83
  980.6 13.8 fusion.82
  1006.0 24.8 %reduce-scatter.13.cloned.1.call-done = f32[192,512]{1,0:T(8,128)} async-done(((f32[1536,512]{1,0:T(8,128)}), f32[192,512]{1,0:T(8,128)}) %reduce-scatter.13.cloned.1.call-update) | async-done | bytes 393232 | tf_op jit(solution)/shard_map/reduce_scatter | solution.py:274
  1030.7 80.0 %reduce-scatter.17.cloned.1.call-done = f32[192,1536]{1,0:T(8,128)} async-done(((f32[1536,1536]{1,0:T(8,128)}), f32[192,1536]{1,0:T(8,128)}) %reduce-scatter.17.cloned.1.call-update) | async-done | bytes 1179664 | tf_op jit(solution)/shard_map/reduce_scatter | solution.py:276
  1110.7 80.0 %reduce-scatter.11.cloned.1.call-done = f32[192,1536]{1,0:T(8,128)} async-done(((f32[1536,1536]{1,0:T(8,128)}), f32[192,1536]{1,0:T(8,128)}) %reduce-scatter.11.cloned.1.call-update) | async-done | bytes 1179664 | tf_op jit(solution)/shard_map/reduce_scatter | solution.py:273
  1191.6 37.9 %reduce-scatter.25.cloned.1.call-done = f32[192,20]{1,0:T(8,128)} async-done(((f32[1536,20]{1,0:T(8,128)}), f32[192,20]{1,0:T(8,128)}) %reduce-scatter.25.cloned.1.call-update) | async-done | bytes 15376
  1236.2 22.8 %all-reduce.4 = (f32[1536]{0:T(1024)S(1)}, f32[1536]{0:T(1024)S(1)}) all-reduce(f32[1536]{0:T(1024)S(1)} %get-tuple-element.14, f32[1536]{0:T(1024)S(1)} %copy-done.47), channel_id=6, replica_groups=mesh['dp'=8,'expert'=4] {'dp'}, use_global_device_ids=true, to_apply=%region_28.29.clone | all-reduce | flops 3072 | bytes 24576
  1259.1 19.6 %all-reduce.5 = (f32[192]{0:T(256)}, f32[192]{0:T(256)}, f32[192,20]{0,1:T(8,128)}) all-reduce(f32[192]{0:T(256)S(1)} %dynamic-slice.3, f32[192]{0:T(256)S(1)} %dynamic-slice.5, f32[192,20]{0,1:T(8,128)S(1)} %copy.133), channel_id=1, replica_groups=mesh['dp'=8,'expert'=4] {'expert'}, use_global_device_ids=true, to_apply=%region_29.30 | all-reduce | flops 4224 | bytes 33792 | tf_op jit(solution)/shard_map/psum | solution.py:281
  1279.9 62.7 %reduce-scatter.23.cloned.1.call-done = f32[5,64,1536]{2,1,0:T(8,128)} async-done(((f32[5,512,1536]{2,1,0:T(8,128)}), f32[5,64,1536]{2,1,0:T(8,128)}) %reduce-scatter.23.cloned.1.call-update) | async-done | bytes 1966096 | tf_op jit(solution)/shard_map/reduce_scatter | solution.py:296
  1342.6 113.3 %reduce-scatter.21.cloned.1.call-done = f32[5,192,512]{2,1,0:T(8,128)} async-done(((f32[5,1536,512]{2,1,0:T(8,128)}), f32[5,192,512]{2,1,0:T(8,128)}) %reduce-scatter.21.cloned.1.call-update) | async-done | bytes 1966096 | tf_op jit(solution)/shard_map/reduce_scatter | solution.py:295
  1455.9 113.1 %reduce-scatter.19.cloned.1.call-done = f32[5,192,512]{2,1,0:T(8,128)} async-done(((f32[5,1536,512]{2,1,0:T(8,128)}), f32[5,192,512]{2,1,0:T(8,128)}) %reduce-scatter.19.cloned.1.call-update) | async-done | bytes 1966096 | tf_op jit(solution)/shard_map/reduce_scatter | solution.py:294
  1569.1 124.8 %all-reduce.10.cloned.1.call-done = (f32[192,1536]{1,0:T(8,128)}, f32[192,512]{1,0:T(8,128)}, f32[192,512]{1,0:T(8,128)}, f32[192,1536]{1,0:T(8,128)}) async-done(((f32[192,1536]{1,0:T(8,128)}, f32[192,512]{1,0:T(8,128)}, f32[192,512]{1,0:T(8,128)}, f32[192,1536]{1,0:T(8,128)}), (f32[192,1536]{1,0:T(8,128)}, f32[192,512]{1,0:T(8,128)}, f32[192,512]{1,0:T(8,128)}, ...) | async-done | bytes 3145744 | tf_op jit(solution)/shard_map/psum | solution.py:281
  (262 shorter events, 219.7 us)
Async XLA Ops:
  7.2 31.3 %all-gather.6.cloned.1.call-start = ((), (), s32[]{:S(2)}) async-start(), calls=%async_computation.12 | async-start | bytes 1769472 | tf_op jit(solution)/shard_map/all_gather | solution.py:94
  8.0 58.2 %all-gather.8.cloned.1.call-start = ((), (), s32[]{:S(2)}) async-start(), calls=%async_computation.13 | async-start | bytes 1769472 | tf_op jit(solution)/shard_map/all_gather | solution.py:93
  8.7 98.3 %all-gather.10.cloned.1.call-start = ((), (), s32[]{:S(2)}) async-start(), calls=%async_computation.14 | async-start | bytes 5308416 | tf_op jit(solution)/shard_map/all_gather | solution.py:92
  9.4 138.2 %all-gather.12.cloned.1.call-start = ((), (), s32[]{:S(2)}) async-start(), calls=%async_computation.15 | async-start | bytes 5308416 | tf_op jit(solution)/shard_map/all_gather | solution.py:95
  30.4 121.2 %copy-start.37 = (f32[1536]{0:T(1024)}, f32[1536]{0:T(1024)S(1)}, u32[]{:S(2)}) copy-start(f32[1536]{0:T(1024)S(1)} %convert_element_type.119) | copy-start | bytes 18436
  37.6 73.7 %copy-start.48 = (f32[128]{0:T(128)}, f32[128]{0:T(128)S(1)}, u32[]{:S(2)}) copy-start(f32[128]{0:T(128)S(1)} %get-tuple-element.53) | copy-start | bytes 1540
  37.6 114.3 %copy-start.54 = (s32[1024]{0:T(1024)}, s32[1024]{0:T(1024)S(1)}, u32[]{:S(2)}) copy-start(s32[1024]{0:T(1024)S(1)} %broadcast_select_fusion) | copy-start | bytes 12292
  37.9 73.5 %copy-start.26 = (f32[128,32]{0,1:T(8,128)}, f32[128,32]{0,1:T(8,128)S(1)}, u32[]{:S(2)}) copy-start(f32[128,32]{0,1:T(8,128)S(1)} %get-tuple-element.48) | copy-start | bytes 49156
  152.0 189.1 %copy-start.7 = (bf16[128,1536]{1,0:T(8,128)(2,1)}, bf16[128,1536]{1,0:T(8,128)(2,1)S(1)}, u32[]{:S(2)}) copy-start(bf16[128,1536]{1,0:T(8,128)(2,1)S(1)} %multiply_convert_fusion.3) | copy-start | bytes 1179652
  325.3 134.6 %all-to-all-start.1 = ((bf16[4,5,96,1536]{3,2,1,0:T(8,128)(2,1)}), bf16[4,5,96,1536]{3,2,1,0:T(8,128)(2,1)}, u32[]{:S(2)}, u32[]{:S(2)}) async-start(bf16[4,5,96,1536]{3,2,1,0:T(8,128)(2,1)} %pad_maximum_fusion), calls=%async_computation.1 | async-start | bytes 11796480 | tf_op jit(solution)/shard_map/all_to_all | solution.py:171
  340.1 119.8 %copy-start.24 = (bf16[1536,20]{0,1:T(8,128)(2,1)}, bf16[1536,20]{0,1:T(8,128)(2,1)S(1)}, u32[]{:S(2)}) copy-start(bf16[1536,20]{0,1:T(8,128)(2,1)S(1)} %reshape.372) | copy-start | bytes 184324
  341.3 118.6 %copy-start.53 = (f32[128]{0:T(128)}, f32[128]{0:T(128)S(1)}, u32[]{:S(2)}) copy-start(f32[128]{0:T(128)S(1)} %reduce_max.19) | copy-start | bytes 1540
  676.5 210.6 %all-to-all-start.3 = ((bf16[5,384,1536]{2,0,1:T(8,128)(2,1)}), bf16[5,384,1536]{2,0,1:T(8,128)(2,1)}, u32[]{:S(2)}, u32[]{:S(2)}) async-start(bf16[5,384,1536]{2,0,1:T(8,128)(2,1)} %copy.106), calls=%async_computation.3 | async-start | bytes 18874368 | tf_op jit(solution)/shard_map/all_to_all | solution.py:213
  682.5 323.5 %reduce-scatter.15.cloned.1.call-start = ((), (), s32[]{:S(2)}) async-start(), calls=%async_computation.18 | async-start | bytes 3538944 | tf_op jit(solution)/shard_map/reduce_scatter | solution.py:275
  683.1 239.9 %copy-start.39 = (f32[128,20]{0,1:T(8,128)}, f32[128,20]{0,1:T(8,128)S(1)}, u32[]{:S(2)}) copy-start(f32[128,20]{0,1:T(8,128)S(1)} %select_reduce_fusion) | copy-start | bytes 30724
  936.3 94.4 %reduce-scatter.13.cloned.1.call-start = ((), (), s32[]{:S(2)}) async-start(), calls=%async_computation.17 | async-start | bytes 3538944 | tf_op jit(solution)/shard_map/reduce_scatter | solution.py:274
  946.5 164.2 %reduce-scatter.17.cloned.1.call-start = ((), (), s32[]{:S(2)}) async-start(), calls=%async_computation.19 | async-start | bytes 10616832 | tf_op jit(solution)/shard_map/reduce_scatter | solution.py:276
  951.5 239.2 %reduce-scatter.11.cloned.1.call-start = ((), (), s32[]{:S(2)}) async-start(), calls=%async_computation.16 | async-start | bytes 10616832 | tf_op jit(solution)/shard_map/reduce_scatter | solution.py:273
  964.1 265.4 %reduce-scatter.25.cloned.1.call-start = ((), (), s32[]{:S(2)}) async-start(), calls=%async_computation.23 | async-start | bytes 884736
  967.2 375.4 %reduce-scatter.23.cloned.1.call-start = ((), (), s32[]{:S(2)}) async-start(), calls=%async_computation.22 | async-start | bytes 17694720 | tf_op jit(solution)/shard_map/reduce_scatter | solution.py:296
  980.4 475.6 %reduce-scatter.21.cloned.1.call-start = ((), (), s32[]{:S(2)}) async-start(), calls=%async_computation.21 | async-start | bytes 17694720 | tf_op jit(solution)/shard_map/reduce_scatter | solution.py:295
  994.5 574.6 %reduce-scatter.19.cloned.1.call-start = ((), (), s32[]{:S(2)}) async-start(), calls=%async_computation.20 | async-start | bytes 17694720 | tf_op jit(solution)/shard_map/reduce_scatter | solution.py:294
  1005.9 224.6 %copy-start.12 = (bf16[128,24,64]{0,2,1:T(8,128)(2,1)S(1)}, bf16[128,24,64]{0,2,1:T(8,128)(2,1)}, u32[]{:S(2)}) copy-start(bf16[128,24,64]{0,2,1:T(8,128)(2,1)} %copy-done.11) | copy-start | bytes 1179652
  1005.9 687.9 %all-reduce.10.cloned.1.call-start = ((), (), s32[]{:S(2)}) async-start(), calls=%async_computation.24 | async-start | bytes 6291456 | tf_op jit(solution)/shard_map/psum | solution.py:281
  (53 other events, 716.8 us)
Sparse Core Ops, SparseCore 0:
  9.9 28.5 all-gather.5
  40.4 25.7 all-gather.7
  68.0 38.9 all-gather.9
  108.7 38.9 all-gather.11
  936.5 44.3 reduce-scatter.14
  984.5 46.1 reduce-scatter.12
  1034.2 76.4 reduce-scatter.16
  1114.2 76.4 reduce-scatter.10
  1194.5 34.9 reduce-scatter.24
  1233.4 109.1 reduce-scatter.22
  1346.7 109.1 reduce-scatter.20
  1459.8 109.1 reduce-scatter.18
  1571.7 122.1 all-reduce.9
